TPU v7x, 32 devices: a whole 2x2x4 slice. The times are simulated.
32 devices in a mesh: grp: 2 (over x), kv: 16 (over z, y, core).
Axes of the slice: x: 2, y: 2, z: 4, core: 2. Of those that a mesh axis runs over, the one named last changes fastest.
Arguments:
- absorbed_query: bfloat16 [8, 128, 576], P('grp', 'kv'), parts along dimension 0, may hold values from -65 to 65
- latent_cache: bfloat16 [8, 32768, 576], P('grp', 'kv'), parts along dimension 0, may hold values from -6 to 6
- slot_position: int32 [8, 32768], P('grp', 'kv'), parts along dimension 0, may hold values from 0 to 32767, as said below
- context_lengths: int32 [8], P('grp'), parts along dimension 0, may hold values from 16384 to 32768, as said below
- value_up: bfloat16 [128, 512, 128], P('kv'), may hold values from -2.09375 to 2.09375
Outputs:
- attended: bfloat16 [8, 16384], P('grp', 'kv'), parts along dimension 0
There are 2 independent parts, one for each index of `grp`. A program takes and returns all parts, laid end to end along the dimension named above; an argument that names none is the same for every part. Nothing has to cross between parts.
Inputs may be any that keep to these rules, and one draw needn't show every extreme that they name: `slot_position`: each row is an ordering of 0 to 32767. `context_lengths`: some request holds exactly 32768 tokens.
All inputs are finite; a program needn't handle non-finite values.
Results may differ from a plain program's by a relative error of at most 0.0095.
Values may be sent and summed in bfloat16 or wider, within the bound.
A program may use at most 64 MiB of HBM per device.

v0:
```python
import functools

import jax
import jax.numpy as jnp
from jax import lax
from jax.experimental import pallas as pl
from jax.experimental.pallas import tpu as pltpu
from jax.sharding import PartitionSpec as P

softmax_scale = 192.0 ** (-0.5)
masked_score = -1e30
MESH = pl.DeviceIdType.MESH
LANES = 128


def merge(parts):
    peak = functools.reduce(jnp.maximum, [lse for _, lse in parts])
    factors = [jnp.exp(lse - peak) for _, lse in parts]
    total = sum(factors[1:], factors[0])
    inverse = 1.0 / total
    mixed = sum(
        [part * (f * inverse) for (part, _), f in zip(parts[1:], factors[1:])],
        parts[0][0] * (factors[0] * inverse),
    )
    return mixed, peak + jnp.log(total)


def packed(mixed, lse):
    lanes = lax.broadcasted_iota(jnp.int32, (mixed.shape[0], LANES), 1)
    high = lse.astype(jnp.bfloat16).astype(jnp.float32)
    rest = lse - high
    middle = rest.astype(jnp.bfloat16).astype(jnp.float32)
    low = rest - middle
    return mixed.astype(jnp.bfloat16), jnp.where(
        lanes == 0, high, jnp.where(lanes == 1, middle, low)
    ).astype(jnp.bfloat16)


def unpacked(ref, latent):
    mixed = ref[:, :latent].astype(jnp.float32)
    tail = ref[:, latent:].astype(jnp.float32)
    return mixed, (tail[:, 0:1] + tail[:, 1:2]) + tail[:, 2:3]


def kernel(
    depth, q_ref, k_hbm, pos_ref, len_ref, w_hbm, out_ref,
    kbuf, wbuf, qall, qrows, keep, keep_lse,
    send1, recv1, send2, recv2, final,
    k_sem, w_sem, qs_sem, qr_sem, s_sem, r_sem,
):
    requests, heads_here, width = q_ref.shape
    latent = wbuf.shape[1]
    devices = 4 * depth
    heads = devices * heads_here
    me = lax.axis_index("kv")
    core, row, level = lax.rem(me, 2), lax.rem(me // 2, 2), me // 4

    def device(dc, dr, dl):
        c = 1 - core if dc else core
        r = 1 - row if dr else row
        l = lax.rem(level + dl, depth) if dl else level
        return {"kv": (l * 2 + r) * 2 + c}

    def slot(dc, dr, dl):
        return (dc * 2 + dr) * depth + dl

    for r in range(requests):
        pltpu.make_async_copy(k_hbm.at[r], kbuf.at[r], k_sem.at[r]).start()
    pltpu.make_async_copy(w_hbm, wbuf, w_sem).start()

    core_peer, row_peer = device(1, 0, 0), device(0, 1, 0)
    level_peers = {k: device(0, 0, k) for k in range(1, depth)}
    owners = {(dr, k): device(0, dr, k) for dr in range(2) for k in range(depth) if dr or k}
    barrier = pltpu.get_barrier_semaphore()
    for peer in [core_peer, row_peer] + list(level_peers.values()):
        pl.semaphore_signal(barrier, inc=1, device_id=peer, device_id_type=MESH)
    pl.semaphore_wait(barrier, depth + 1)

    sends, arrivals = [], {}

    def send_query(src, place, r, peer):
        copy = pltpu.make_async_remote_copy(
            src_ref=src.at[r], dst_ref=qall.at[place, r],
            send_sem=qs_sem.at[place, r], recv_sem=qr_sem.at[place, r],
            device_id=peer, device_id_type=MESH,
        )
        copy.start()
        sends.append(copy)
        arrivals[place, r] = copy

    def gather0(r):
        for k in range(1, depth):
            send_query(q_ref, slot(0, 0, depth - k), r, level_peers[k])
        send_query(q_ref, slot(0, 1, 0), r, row_peer)
        send_query(q_ref, slot(1, 0, 0), r, core_peer)

    def gather1(r):
        for k in range(1, depth):
            arrivals[slot(0, 0, k), r].wait_recv()
            send_query(qall.at[slot(0, 0, k)], slot(0, 1, k), r, row_peer)
            send_query(qall.at[slot(0, 0, k)], slot(1, 0, k), r, core_peer)

    def gather2(r):
        for k in range(depth):
            arrivals[slot(0, 1, k), r].wait_recv()
            send_query(qall.at[slot(0, 1, k)], slot(1, 1, k), r, core_peer)

    def gather3(r):
        for dr in range(2):
            for k in range(depth):
                arrivals[slot(1, dr, k), r].wait_recv()

    for r in range(requests):
        gather0(r)
    qall[0] = q_ref[...]

    def attend(r, between=None):
        for place in range(devices):
            qrows[place * heads_here : (place + 1) * heads_here, :] = qall[place, r].astype(jnp.float32)
        pltpu.make_async_copy(k_hbm.at[r], kbuf.at[r], k_sem.at[r]).wait()
        queries = qrows[...].astype(jnp.bfloat16)
        scores = lax.dot_general(
            queries, kbuf[r], (((1,), (0,)), ((), ())), preferred_element_type=jnp.float32
        )
        usable = pos_ref[r : r + 1, :] < len_ref[r]
        scores = jnp.where(usable, scores, masked_score)
        peak = jnp.max(scores, axis=1, keepdims=True)
        weights = jnp.exp((scores - peak) * softmax_scale)
        total = jnp.sum(weights, axis=1, keepdims=True)
        if between is not None:
            between()
        mixed = lax.dot_general(
            weights.astype(jnp.bfloat16),
            kbuf[r, :latent, :],
            (((1,), (1,)), ((), ())),
            preferred_element_type=jnp.float32,
        )
        return mixed * (1.0 / total), peak * softmax_scale + jnp.log(total)

    def send_part(src, dst, number, r, peer):
        copy = pltpu.make_async_remote_copy(
            src_ref=src, dst_ref=dst,
            send_sem=s_sem.at[number, r], recv_sem=r_sem.at[number, r],
            device_id=peer, device_id_type=MESH,
        )
        copy.start()
        sends.append(copy)
        return copy

    half = heads // 2
    first, second = {}, {}

    def reduce1(r):
        mixed, lse = attend(r, functools.partial(reduce2, r - 1) if r else None)
        values, tail = packed(mixed[half:], lse[half:])
        send1[r, :, :latent] = values
        send1[r, :, latent:] = tail
        first[r] = send_part(send1.at[r], recv1.at[r], 0, r, core_peer)
        keep[r] = mixed[:half]
        keep_lse[r] = jnp.broadcast_to(lse[:half], (half, LANES))

    def reduce2(r):
        first[r].wait_recv()
        mixed, lse = merge([(keep[r], keep_lse[r, :, 0:1]), unpacked(recv1.at[r], latent)])
        values, tail = packed(mixed, lse)
        for dr, k in owners:
            place = dr * depth + k
            rows = slice(place * heads_here, (place + 1) * heads_here)
            send2[r, place, :, :latent] = values[rows]
            send2[r, place, :, latent:] = tail[rows]
        for dr, k in sorted(owners, key=lambda o: -(o[0] + min(o[1], depth - o[1]))):
            place, there = dr * depth + k, dr * depth + (depth - k) % depth
            second[r, there] = send_part(
                send2.at[r, place], recv2.at[r, there], there, r, owners[dr, k]
            )
        keep[r, :heads_here] = mixed[:heads_here]
        keep_lse[r, :heads_here] = jnp.broadcast_to(lse[:heads_here], (heads_here, LANES))

    def reduce3(r):
        parts = [(keep[r, :heads_here], keep_lse[r, :heads_here, 0:1])]
        for place in range(1, 2 * depth):
            second[r, place].wait_recv()
        for place in range(1, 2 * depth):
            parts.append(unpacked(recv2.at[r, place], latent))
        final[r] = merge(parts)[0]

    order = [(gather1, 0), (gather1, 1), (gather2, 0), (gather1, 2), (gather2, 1), (gather3, 0)]
    order = [item for item in order if item[1] < requests]
    for r in range(requests):
        order.append((reduce1, r))
        later = [(gather1, r + 3), (gather2, r + 2), (gather3, r + 1)]
        order += [item for item in later if item[1] < requests]
        if r > 1:
            order.append((reduce3, r - 2))
    order += [(reduce2, requests - 1)]
    order += [(reduce3, r) for r in range(max(requests - 2, 0), requests)]
    for stage, r in order:
        stage(r)

    pltpu.make_async_copy(w_hbm, wbuf, w_sem).wait()
    for h in range(heads_here):
        rows = final[:, h, :].astype(jnp.bfloat16)
        out_ref[:, h * wbuf.shape[2] : (h + 1) * wbuf.shape[2]] = jnp.dot(
            rows, wbuf[h], preferred_element_type=jnp.float32
        ).astype(out_ref.dtype)
    for copy in sends:
        copy.wait_send()


def shards(devices, absorbed_query, latent_cache, slot_position, context_lengths, value_up):
    depth = devices // 4
    requests, heads_here, width = absorbed_query.shape
    slots = latent_cache.shape[1]
    latent, value = value_up.shape[1:]
    heads = devices * heads_here
    wide = latent + LANES
    half = heads // 2
    vmem = pl.BlockSpec(memory_space=pltpu.VMEM)
    hbm = pl.BlockSpec(memory_space=pltpu.HBM)
    bf16, f32 = jnp.bfloat16, jnp.float32
    return pl.pallas_call(
        functools.partial(kernel, depth),
        out_shape=jax.ShapeDtypeStruct((requests, heads_here * value), bf16),
        in_specs=[vmem, hbm, vmem, pl.BlockSpec(memory_space=pltpu.SMEM), hbm],
        out_specs=vmem,
        scratch_shapes=[
            pltpu.VMEM((requests, width, slots), bf16),
            pltpu.VMEM(value_up.shape, bf16),
            pltpu.VMEM((devices, requests, heads_here, width), bf16),
            pltpu.VMEM((heads, width), f32),
            pltpu.VMEM((requests, half, latent), f32),
            pltpu.VMEM((requests, half, LANES), f32),
            pltpu.VMEM((requests, half, wide), bf16),
            pltpu.VMEM((requests, half, wide), bf16),
            pltpu.VMEM((requests, 2 * depth, heads_here, wide), bf16),
            pltpu.VMEM((requests, 2 * depth, heads_here, wide), bf16),
            pltpu.VMEM((requests, heads_here, latent), f32),
            pltpu.SemaphoreType.DMA((requests,)),
            pltpu.SemaphoreType.DMA,
            pltpu.SemaphoreType.DMA((devices, requests)),
            pltpu.SemaphoreType.DMA((devices, requests)),
            pltpu.SemaphoreType.DMA((2 * depth, requests)),
            pltpu.SemaphoreType.DMA((2 * depth, requests)),
        ],
        compiler_params=pltpu.CompilerParams(
            collective_id=0, has_side_effects=True, vmem_limit_bytes=56 * 1024 * 1024
        ),
        name="attention_step",
    )(absorbed_query, jnp.swapaxes(latent_cache, 1, 2), slot_position, context_lengths, value_up)


def solution(mesh):
    return jax.shard_map(
        functools.partial(shards, mesh.shape["kv"]),
        mesh=mesh,
        in_specs=(
            P("grp", "kv", None),
            P("grp", "kv", None),
            P("grp", "kv"),
            P("grp"),
            P("kv", None, None),
        ),
        out_specs=P("grp", "kv"),
        check_vma=False,
    )
```

profile of v0, /device:TPU:0, one launch (start us, length us, event | category | flops | bytes accessed | tf_op | source)
XLA Modules:
  0.0 32.4 jit_solution(195926943175710418)
XLA Ops:
  0.0 31.1 %attention_step.1 = bf16[4,1024]{1,0:T(4,128)(2,1)} custom-call(bf16[4,8,576]{2,1,0:T(8,128)(2,1)} %q_ref.1, bf16[4,576,2048]{2,1,0:T(8,128)(2,1)} %bitcast.1, s32[4,2048]{1,0:T(4,128)} %pos_ref.1, s32[4]{0:T(128)} %len_ref.1, bf16[8,512,128]{2,1,0:T(8,128)(2,1)} %w_hbm.1), custom_call_target="tpu_custom_call" | custom-call | tf_op jit(solution)/shard_map/attention_step/pallas_call | solution.py:221
  31.1 1.3 %copy.7 = bf16[4,1024]{1,0:T(4,128)(2,1)} copy(bf16[4,1024]{1,0:T(4,128)(2,1)} %attention_step.1) | data formatting | bytes 16384
where the time goes:
time: 32.6 us; the launch traced here: 32.4 us
  Pallas kernels  31.1 us (95%)
  local copies, waits for them, and re-layouts  1.3 us (4%)
    pallas_call x1, Pallas kernels, shards(): pl.pallas_call(functools.partial(kernel, depth), out_shape=jax.ShapeDtype...  31.1 us
    unnamed x1, local copies, waits for them, and re-layouts  1.3 us

commit v1 on v0

v1 whole, which is shorter than its diff:
```python
import functools
import math

import jax
import jax.numpy as jnp
from jax import lax
from jax.experimental import pallas as pl
from jax.experimental.pallas import tpu as pltpu
from jax.sharding import PartitionSpec as P

softmax_scale = 192.0 ** (-0.5)
LOG2E = math.log2(math.e)
masked_score = -1e30
MESH = pl.DeviceIdType.MESH
LANES = 128


def packed(mixed, lse):
    lanes = lax.broadcasted_iota(jnp.int32, (mixed.shape[0], LANES), 1)
    high = lse.astype(jnp.bfloat16).astype(jnp.float32)
    rest = lse - high
    middle = rest.astype(jnp.bfloat16).astype(jnp.float32)
    low = rest - middle
    return mixed.astype(jnp.bfloat16), jnp.where(
        lanes == 0, high, jnp.where(lanes == 1, middle, low)
    ).astype(jnp.bfloat16)


def unpacked(ref, latent):
    mixed = ref[:, :latent].astype(jnp.float32)
    tail = ref[:, latent:].astype(jnp.float32)
    return mixed, (tail[:, 0:1] + tail[:, 1:2]) + tail[:, 2:3]


def kernel(
    chips, q_hbm, k_hbm, pos_hbm, len_hbm, w_hbm, out_ref,
    kbuf, wbuf, pos_ref, len_ref, qall, qrows, keep, keep_lse,
    send1, recv1, send2, recv2, lse_out, lse_in, final,
    k_sem, w_sem, pos_sem, len_sem, own_sem,
    q_send, q_recv, relay_send, relay_recv,
    half_send, half_recv, part_send, part_recv, lse_send, lse_recv,
):
    requests, heads_here, width = q_hbm.shape
    slots = kbuf.shape[2]
    latent = wbuf.shape[1]
    half = chips * heads_here
    me = lax.axis_index("kv")
    core, chip = lax.rem(me, 2), me // 2
    partner = {"kv": chip * 2 + 1 - core}
    others = []
    for i in range(chips - 1):
        there = i + (chip <= i).astype(jnp.int32)
        others.append((there, {"kv": there * 2 + core}))

    def remote(src, dst, send_sem, recv_sem, peer):
        pltpu.make_async_remote_copy(
            src_ref=src, dst_ref=dst, send_sem=send_sem, recv_sem=recv_sem,
            device_id=peer, device_id_type=MESH,
        ).start()

    def landed(ref, sem):
        pltpu.make_async_copy(ref, ref, sem).wait()

    barrier = pltpu.get_barrier_semaphore()
    for peer in [partner] + [peer for _, peer in others]:
        pl.semaphore_signal(barrier, inc=1, device_id=peer, device_id_type=MESH)
    for r in range(requests):
        pltpu.make_async_copy(q_hbm.at[r], qall.at[r, 0, chip], own_sem.at[r]).start()
    pltpu.make_async_copy(pos_hbm, pos_ref, pos_sem).start()
    pltpu.make_async_copy(len_hbm, len_ref, len_sem).start()
    pl.semaphore_wait(barrier, chips)

    for r in range(requests):
        for _, peer in others:
            remote(q_hbm.at[r], qall.at[r, 0, chip], q_send, q_recv.at[r], peer)
    for r in range(requests):
        pltpu.make_async_copy(k_hbm.at[r], kbuf.at[r], k_sem.at[r]).start()
    pltpu.make_async_copy(w_hbm, wbuf, w_sem).start()
    landed(pos_ref, pos_sem)
    pltpu.make_async_copy(len_hbm, len_ref, len_sem).wait()

    def relay(r):
        landed(qall.at[r, 0, chip], own_sem.at[r])
        landed(qall.at[r, 0, pl.ds(0, chips - 1)], q_recv.at[r])
        remote(qall.at[r, 0], qall.at[r, 1], relay_send, relay_recv.at[r], partner)

    def attend(r):
        landed(qall.at[r, 1], relay_recv.at[r])
        if heads_here % 8 == 0:
            queries = qall[r].astype(jnp.float32).reshape(2 * half, width)
        else:
            for c in range(2):
                for place in range(chips):
                    first = c * half + place * heads_here
                    qrows[first : first + heads_here, :] = qall[r, c, place].astype(jnp.float32)
            queries = qrows[...]
        queries = queries.astype(jnp.bfloat16)
        pltpu.make_async_copy(k_hbm.at[r], kbuf.at[r], k_sem.at[r]).wait()
        cut = slots // 2
        if cut % LANES:
            spans = [(0, slots)]
        else:
            spans = [(0, cut), (cut, slots)]

        def scored(span):
            scores = lax.dot_general(
                queries, kbuf[r, :, span[0] : span[1]],
                (((1,), (0,)), ((), ())), preferred_element_type=jnp.float32,
            )
            usable = pos_ref[r : r + 1, span[0] : span[1]] < len_ref[r]
            return jnp.where(usable, scores, masked_score)

        parts = []
        coming = scored(spans[0])
        for n, span in enumerate(spans):
            scores = coming
            if n + 1 < len(spans):
                coming = scored(spans[n + 1])
            peak = jnp.max(scores, axis=1, keepdims=True)
            weights = jnp.exp2((scores - peak) * (softmax_scale * LOG2E))
            total = jnp.sum(weights, axis=1, keepdims=True)
            mixed = lax.dot_general(
                weights.astype(jnp.bfloat16), kbuf[r, :latent, span[0] : span[1]],
                (((1,), (1,)), ((), ())), preferred_element_type=jnp.float32,
            )
            parts.append((mixed, peak, total))
        peak = functools.reduce(jnp.maximum, [p for _, p, _ in parts])
        factors = [jnp.exp2((p - peak) * (softmax_scale * LOG2E)) for _, p, _ in parts]
        total = sum(f * t for f, (_, _, t) in zip(factors, parts))
        inverse = 1.0 / total
        mixed = sum(m * (f * inverse) for f, (m, _, _) in zip(factors, parts))
        return mixed, peak * softmax_scale + jnp.log(total)

    def reduce1(r):
        mixed, lse = attend(r)
        values, tail = packed(mixed[half:], lse[half:])
        send1[r, :, :latent] = values
        send1[r, :, latent:] = tail
        remote(send1.at[r], recv1.at[r], half_send, half_recv.at[r], partner)
        keep[r] = mixed[:half]
        keep_lse[r] = jnp.broadcast_to(lse[:half], (half, LANES))

    def reduce2(r):
        landed(recv1.at[r], half_recv.at[r])
        there, there_lse = unpacked(recv1.at[r], latent)
        here_lse = keep_lse[r, :, 0:1]
        peak = jnp.maximum(here_lse, there_lse)
        here_factor, there_factor = jnp.exp(here_lse - peak), jnp.exp(there_lse - peak)
        total = here_factor + there_factor
        inverse = 1.0 / total
        mixed = keep[r] * (here_factor * inverse) + there * (there_factor * inverse)
        lse = peak + jnp.log(total)
        diagonal = lax.broadcasted_iota(jnp.int32, (half, LANES), 0) == lax.broadcasted_iota(
            jnp.int32, (half, LANES), 1
        )
        row = jnp.sum(jnp.where(diagonal, lse, 0.0), axis=0, keepdims=True)
        lse_out[r] = row
        for place in range(chips):
            send2[r, place] = mixed[place * heads_here : (place + 1) * heads_here].astype(jnp.bfloat16)
        for place, peer in others:
            remote(send2.at[r, place], recv2.at[r, chip], part_send, part_recv.at[r], peer)
            remote(lse_out.at[r], lse_in.at[r, chip], lse_send, lse_recv.at[r], peer)
        recv2[r, chip] = send2[r, chip]
        lse_in[r, chip] = row

    def reduce3(r):
        landed(lse_in.at[r, pl.ds(0, chips - 1)], lse_recv.at[r])
        rows = [lse_in[r, place] for place in range(chips)]
        peak = functools.reduce(jnp.maximum, rows)
        factors = [jnp.exp(row - peak) for row in rows]
        inverse = 1.0 / sum(factors[1:], factors[0])
        mine = lax.broadcasted_iota(jnp.int32, (heads_here, LANES), 1) == (
            lax.broadcasted_iota(jnp.int32, (heads_here, LANES), 0) + chip * heads_here
        )
        shares = [
            jnp.sum(jnp.where(mine, f * inverse, 0.0), axis=1, keepdims=True) for f in factors
        ]
        landed(recv2.at[r, pl.ds(0, chips - 1)], part_recv.at[r])
        mixed = recv2[r, 0].astype(jnp.float32) * shares[0]
        for place in range(1, chips):
            mixed = mixed + recv2[r, place].astype(jnp.float32) * shares[place]
        final[r] = mixed

    for r in range(min(2, requests)):
        relay(r)
    for r in range(requests):
        reduce1(r)
        if r + 2 < requests:
            relay(r + 2)
        if r:
            reduce2(r - 1)
    reduce2(requests - 1)
    landed(qall.at[:, 0, pl.ds(0, chips - 1)], q_send)
    landed(qall.at[:, 0], relay_send)
    landed(send1, half_send)
    pltpu.make_async_copy(w_hbm, wbuf, w_sem).wait()
    for r in range(requests):
        reduce3(r)
    value = wbuf.shape[2]
    for h in range(heads_here):
        rows = final[:, h, :].astype(jnp.bfloat16)
        out_ref[:, h * value : (h + 1) * value] = jnp.dot(
            rows, wbuf[h], preferred_element_type=jnp.float32
        ).astype(out_ref.dtype)
    landed(recv2.at[:, pl.ds(0, chips - 1)], part_send)
    landed(lse_in.at[:, pl.ds(0, chips - 1)], lse_send)


def shards(devices, absorbed_query, latent_cache, slot_position, context_lengths, value_up):
    chips = devices // 2
    requests, heads_here, width = absorbed_query.shape
    slots = latent_cache.shape[1]
    latent, value = value_up.shape[1:]
    heads = devices * heads_here
    wide = latent + LANES
    half = heads // 2
    hbm = pl.BlockSpec(memory_space=pltpu.HBM)
    bf16, f32 = jnp.bfloat16, jnp.float32
    dma = pltpu.SemaphoreType.DMA
    each = dma((requests,))
    return pl.pallas_call(
        functools.partial(kernel, chips),
        out_shape=pltpu.VMEM((requests, heads_here * value), bf16),
        in_specs=[hbm] * 5,
        out_specs=pl.BlockSpec(memory_space=pltpu.VMEM),
        scratch_shapes=[
            pltpu.VMEM((requests, width, slots), bf16),
            pltpu.VMEM(value_up.shape, bf16),
            pltpu.VMEM(slot_position.shape, jnp.int32),
            pltpu.SMEM(context_lengths.shape, jnp.int32),
            pltpu.VMEM((requests, 2, chips, heads_here, width), bf16),
            pltpu.VMEM((heads if heads_here % 8 else 8, width), f32),
            pltpu.VMEM((requests, half, latent), f32),
            pltpu.VMEM((requests, half, LANES), f32),
            pltpu.VMEM((requests, half, wide), bf16),
            pltpu.VMEM((requests, half, wide), bf16),
            pltpu.VMEM((requests, chips, heads_here, latent), bf16),
            pltpu.VMEM((requests, chips, heads_here, latent), bf16),
            pltpu.VMEM((requests, 1, LANES), f32),
            pltpu.VMEM((requests, chips, 1, LANES), f32),
            pltpu.VMEM((requests, heads_here, latent), f32),
            each, dma, dma, dma, each,
            dma, each, dma, each,
            dma, each, dma, each, dma, each,
        ],
        compiler_params=pltpu.CompilerParams(
            collective_id=0, has_side_effects=True, vmem_limit_bytes=56 * 1024 * 1024
        ),
        name="attention_step",
    )(absorbed_query, jnp.swapaxes(latent_cache, 1, 2), slot_position, context_lengths, value_up)


def solution(mesh):
    return jax.shard_map(
        functools.partial(shards, mesh.shape["kv"]),
        mesh=mesh,
        in_specs=(
            P("grp", "kv", None),
            P("grp", "kv", None),
            P("grp", "kv"),
            P("grp"),
            P("kv", None, None),
        ),
        out_specs=P("grp", "kv"),
        check_vma=False,
    )
```

time: 32.6 us -> 26.8 us (0.82)
  Pallas kernels: 31.1 us -> 26 us
  local copies, waits for them, and re-layouts: 1.3 us -> 0.6 us
    pallas_call x1, Pallas kernels: 31.1 us -> 26 us  [shards(): pl.pallas_call(functools.partial(kernel, chips), out_shape=pltpu.VMEM((re...]
    unnamed x1, local copies, waits for them, and re-layouts: 1.3 us -> 0.6 us
where the time goes in v1:
time: 26.8 us; the launch traced here: 26.6 us
  Pallas kernels  26 us (97%)
  local copies, waits for them, and re-layouts  0.6 us (2%)
    pallas_call x1, Pallas kernels, shards(): pl.pallas_call(functools.partial(kernel, chips), out_shape=pltpu.VMEM((re...  26 us
    unnamed x1, local copies, waits for them, and re-layouts  0.6 us

profile of v1, /device:TPU:0, one launch (start us, length us, event | category | flops | bytes accessed | tf_op | source)
XLA Modules:
  0.0 26.6 jit_solution(2609358724907270214)
XLA Ops:
  0.0 26.0 %attention_step.1 = bf16[4,1024]{1,0:T(4,128)(2,1)S(1)} custom-call(bf16[4,8,576]{2,1,0:T(8,128)(2,1)} %q_hbm.1, bf16[4,576,2048]{2,1,0:T(8,128)(2,1)} %bitcast.1, s32[4,2048]{1,0:T(4,128)} %pos_hbm.1, s32[4]{0:T(128)} %len_hbm.1, bf16[8,512,128]{2,1,0:T(8,128)(2,1)} %w_hbm.1), custom_call_target="tpu_custom_call" | custom-call | tf_op jit(solution)/shard_map/attention_step/pallas_call | solution.py:221
  26.0 0.6 %copy.7 = bf16[4,1024]{1,0:T(4,128)(2,1)} copy(bf16[4,1024]{1,0:T(4,128)(2,1)S(1)} %attention_step.1) | data formatting | bytes 16384
